TPU v7x, 128 devices: a whole 4x4x4 slice. The times are simulated.
128 devices in a mesh: seq: 32 (over z, x, core), mp: 4 (over y).
Axes of the slice: x: 4, y: 4, z: 4, core: 2. Of those that a mesh axis runs over, the one named last changes fastest.
Arguments:
- queries: bfloat16 [32768, 4096], P('seq', 'mp'), may hold values from -20 to 20
- image_keys: bfloat16 [32, 768, 512], P('seq', None, 'mp'), may hold values from -5 to 5
- image_values: bfloat16 [32, 768, 512], P('seq', None, 'mp'), may hold values from -80 to 80
- span_tiles: int32 [1024, 1], P('seq'), may hold values from 0 to 31; in each aligned block of 32 rows (0 to 31, 32 to 63, ...) at most 2 rows name the same one
- gate_logit: float32 [1], replicated, may hold values from 0.3 to 1.5
- cotangent: bfloat16 [32768, 4096], P('seq', 'mp'), may hold values from -36 to 36
Outputs:
- attended: bfloat16 [32768, 4096], P('seq', 'mp')
- query_grad: bfloat16 [32768, 4096], P('seq', 'mp')
- key_grad: bfloat16 [32, 768, 512], P('seq', None, 'mp')
- value_grad: bfloat16 [32, 768, 512], P('seq', None, 'mp')
- gate_grad: float32 [1], replicated
Inputs may be any that keep to these rules, and one draw needn't show every extreme that they name: `span_tiles`: among the 32 spans of one index of seq, at most 2 reference the same tile, and that bound is reached; every tile is referenced by some span.
All inputs are finite; a program needn't handle non-finite values.
Results may differ from a plain program's by a relative error of at most 0.012.
The roundings to bfloat16 on the way count: a program that leaves them out, or rounds other values in their place, can miss the bound.
Values may be sent and summed in bfloat16 or wider, within the bound.
A program may use at most 192 MiB of HBM per device.

v0:
```python
import math

import jax
import jax.numpy as jnp
from jax import lax
from jax.sharding import PartitionSpec as P

HEAD = 128


def body(queries, image_keys, image_values, span_tiles, gate_logit, cotangent):
    seq_count = lax.axis_size("seq")
    mp_count = lax.axis_size("mp")
    span_count = span_tiles.shape[0]
    tok_count, columns = queries.shape
    kv_columns = image_keys.shape[2]
    span_len = tok_count // span_count
    head_count = columns // HEAD
    kv_count = kv_columns // HEAD
    group = head_count // kv_count
    image_len = image_keys.shape[1]
    score_scale = 1.0 / math.sqrt(HEAD)
    gate_tanh = jnp.tanh(gate_logit[0])
    owners = span_tiles[:, 0]
    attn_grad = (gate_tanh * cotangent.astype(jnp.float32)).astype(jnp.bfloat16)
    capacity = max(2, 2 * span_count // seq_count)
    slot_count = seq_count * capacity
    row_count = slot_count * span_len
    block_rows = min(512, row_count)
    block_count = row_count // block_rows
    owner_hits = (owners[:, None] == jnp.arange(seq_count, dtype=jnp.int32)[None, :]).astype(
        jnp.float32
    )
    earlier = (jnp.arange(span_count)[:, None] > jnp.arange(span_count)[None, :]).astype(
        jnp.float32
    )
    before = jnp.dot(earlier, owner_hits, precision=lax.Precision.HIGHEST)
    slot_index = jnp.sum(before * owner_hits, axis=1).astype(jnp.int32)
    target = owners * capacity + slot_index
    dispatch = (jnp.arange(slot_count, dtype=jnp.int32)[:, None] == target[None, :]).astype(
        jnp.bfloat16
    )
    keys_heads = image_keys[0].reshape(image_len, kv_count, HEAD)
    values_heads = image_values[0].reshape(image_len, kv_count, HEAD)
    lane_shape = (seq_count, capacity * span_len, columns)

    def send_out(row_data):
        packed = jnp.dot(
            dispatch,
            row_data.reshape(span_count, span_len * columns),
            preferred_element_type=jnp.float32,
        )
        return packed.astype(jnp.bfloat16).reshape(lane_shape)

    def bring_home(packed):
        flat_rows = packed.reshape(slot_count, span_len * columns)
        returned = lax.dot_general(
            dispatch, flat_rows, (((0,), (0,)), ((), ())), preferred_element_type=jnp.float32
        )
        return returned.astype(jnp.bfloat16).reshape(tok_count, columns)

    def softmax_rows(query_block):
        scores = (
            jnp.einsum(
                "bngd,knd->ngbk", query_block, keys_heads, preferred_element_type=jnp.float32
            )
            * score_scale
        )
        row_max = jnp.max(scores, axis=3, keepdims=True)
        expo_terms = jnp.exp(scores - row_max)
        return expo_terms / jnp.sum(expo_terms, axis=3, keepdims=True)

    query_rows = lax.all_to_all(
        send_out(queries), "seq", split_axis=0, concat_axis=0, tiled=True
    ).reshape(row_count, columns)

    def attend_block(query_block):
        shaped = query_block.reshape(block_rows, kv_count, group, HEAD)
        weights = softmax_rows(shaped).astype(jnp.bfloat16)
        result = jnp.einsum(
            "ngbk,knd->bngd", weights, values_heads, preferred_element_type=jnp.float32
        )
        return result.astype(jnp.bfloat16).reshape(block_rows, columns)

    blocks = lax.map(attend_block, query_rows.reshape(block_count, block_rows, columns))
    output_rows = blocks.reshape(row_count, columns)
    attended_home = bring_home(
        lax.all_to_all(
            output_rows.reshape(lane_shape), "seq", split_axis=0, concat_axis=0, tiled=True
        )
    )
    grad_rows = lax.all_to_all(
        send_out(attn_grad), "seq", split_axis=0, concat_axis=0, tiled=True
    ).reshape(row_count, columns)

    def grad_step(accums, pieces):
        key_acc, value_acc = accums
        query_block = pieces[0].reshape(block_rows, kv_count, group, HEAD)
        output_block = pieces[1].reshape(block_rows, kv_count, group, HEAD)
        grad_block = pieces[2].reshape(block_rows, kv_count, group, HEAD)
        weights = softmax_rows(query_block)
        weights_b = weights.astype(jnp.bfloat16)
        row_delta = jnp.sum(
            grad_block.astype(jnp.float32) * output_block.astype(jnp.float32), axis=3
        )
        delta_t = jnp.transpose(row_delta, (1, 2, 0))[:, :, :, None]
        prob_grad = jnp.einsum(
            "bngd,knd->ngbk", grad_block, values_heads, preferred_element_type=jnp.float32
        )
        dscore = (weights * (prob_grad - delta_t) * score_scale).astype(jnp.bfloat16)
        query_grads = jnp.einsum(
            "ngbk,knd->bngd", dscore, keys_heads, preferred_element_type=jnp.float32
        )
        key_acc = key_acc + jnp.einsum(
            "ngbk,bngd->knd", dscore, query_block, preferred_element_type=jnp.float32
        )
        value_acc = value_acc + jnp.einsum(
            "ngbk,bngd->knd", weights_b, grad_block, preferred_element_type=jnp.float32
        )
        return ((key_acc, value_acc), query_grads.astype(jnp.bfloat16).reshape(block_rows, columns))

    start = (
        jnp.zeros((image_len, kv_count, HEAD), jnp.float32),
        jnp.zeros((image_len, kv_count, HEAD), jnp.float32),
    )
    stacked = (
        query_rows.reshape(block_count, block_rows, columns),
        output_rows.reshape(block_count, block_rows, columns),
        grad_rows.reshape(block_count, block_rows, columns),
    )
    (key_acc, value_acc), grads = lax.scan(grad_step, start, stacked)
    query_grads, key_acc, value_acc = (grads.reshape(row_count, columns), key_acc, value_acc)
    query_grad_home = bring_home(
        lax.all_to_all(
            query_grads.reshape(lane_shape), "seq", split_axis=0, concat_axis=0, tiled=True
        )
    )
    key_grad = key_acc.astype(jnp.bfloat16).reshape(1, image_len, kv_columns)
    value_grad = value_acc.astype(jnp.bfloat16).reshape(1, image_len, kv_columns)
    attended = (gate_tanh * attended_home.astype(jnp.float32)).astype(jnp.bfloat16)
    partial_value = jnp.sum(cotangent.astype(jnp.float32) * attended_home.astype(jnp.float32))
    grand_total = lax.psum(partial_value, ("seq", "mp"))
    normaliser = math.sqrt(tok_count * seq_count * columns * mp_count)
    gate_grad = ((1.0 - gate_tanh * gate_tanh) * grand_total / normaliser).reshape(1)
    return (attended, query_grad_home, key_grad, value_grad, gate_grad)


def solution(mesh):
    placed = (
        P("seq", "mp"),
        P("seq", None, "mp"),
        P("seq", None, "mp"),
        P("seq", None),
        P(),
        P("seq", "mp"),
    )
    return jax.shard_map(
        body,
        mesh=mesh,
        in_specs=placed,
        out_specs=(P("seq", "mp"), P("seq", "mp"), P("seq", None, "mp"), P("seq", None, "mp"), P()),
        check_vma=False,
    )
```

profile of v0, /device:TPU:1, one launch (start us, length us, event | category | flops | bytes accessed | tf_op | source)
XLA Modules:
  0.0 520.4 jit_solution(7391767489095752124)
XLA Ops:
  2.2 2.9 reshape.173
  5.1 3.2 convolution_convert_fusion.2
  8.3 7.4 %reshape.174 = bf16[32,64,1024]{2,1,0:T(8,128)(2,1)} reshape(bf16[64,32768]{1,0:T(8,128)(2,1)} %convolution_convert_fusion.2) | data formatting | bytes 8388608 | tf_op jit(solution)/shard_map/reshape | solution.py:53
  15.7 9.6 %all-to-all-start = ((bf16[32,64,1024]{2,1,0:T(8,128)(2,1)}), bf16[32,64,1024]{2,1,0:T(8,128)(2,1)}, u32[]{:S(2)}, u32[]{:S(2)}) async-start(bf16[32,64,1024]{2,1,0:T(8,128)(2,1)} %reshape.174), calls=%async_computation | async-start | bytes 8388608 | tf_op jit(solution)/shard_map/all_to_all | solution.py:73
  27.4 48.2 %all-to-all-done = bf16[32,64,1024]{2,1,0:T(8,128)(2,1)} async-done(((bf16[32,64,1024]{2,1,0:T(8,128)(2,1)}), bf16[32,64,1024]{2,1,0:T(8,128)(2,1)}, u32[]{:S(2)}, u32[]{:S(2)}) %all-to-all-start) | async-done | bytes 4194336 | tf_op jit(solution)/shard_map/all_to_all | solution.py:73
  75.6 6.2 %copy.36 = bf16[4,512,1024]{1,2,0:T(8,128)(2,1)} copy(bf16[4,512,1024]{2,1,0:T(8,128)(2,1)} %bitcast.17) | data formatting | bytes 8388608 | tf_op jit(solution)/shard_map/while | solution.py:85
  81.8 45.6 %while.25 = (s32[]{:T(128)}, bf16[4,512,1024]{1,2,0:T(8,128)(2,1)}, bf16[4,512,1024]{1,2,0:T(8,128)(2,1)}, bf16[768,1,128]{2,0,1:T(8,128)(2,1)S(1)}, bf16[768,1,128]{0,2,1:T(8,128)(2,1)S(1)}, /*index=5*/s32[]{:T(128)}) while((s32[]{:T(128)}, bf16[4,512,1024]{1,2,0:T(8,128)(2,1)}, bf16[4,512,1024]{1,2,0:T(8,128)(2,1)}, ...), condition=%wide.region_4.5_spmd, body=%wide.region_1.4_spmd.sunk | while | flops 1639440384 | bytes 44515412 | solution.py:85
  85.0 3.0 fusion.77
  87.9 4.1 fusion.78
  96.4 3.0 fusion.77
  99.3 4.1 fusion.78
  107.8 3.0 fusion.77
  110.8 4.1 fusion.78
  119.2 3.0 fusion.77
  122.2 4.1 fusion.78
  127.4 6.4 %copy.39 = bf16[4,512,1024]{2,1,0:T(8,128)(2,1)} copy(bf16[4,512,1024]{1,2,0:T(8,128)(2,1)} %get-tuple-element.303) | data formatting | bytes 8388608 | tf_op jit(solution)/shard_map/while | solution.py:85
  133.7 8.0 %all-to-all-start.1 = ((bf16[32,64,1024]{2,1,0:T(8,128)(2,1)}), bf16[32,64,1024]{2,1,0:T(8,128)(2,1)}, u32[]{:S(2)}, u32[]{:S(2)}) async-start(bf16[32,64,1024]{2,1,0:T(8,128)(2,1)} %bitcast.230), calls=%async_computation.1 | async-start | bytes 8388608 | tf_op jit(solution)/shard_map/all_to_all | solution.py:88
  142.4 49.7 %all-to-all-done.1 = bf16[32,64,1024]{2,1,0:T(8,128)(2,1)} async-done(((bf16[32,64,1024]{2,1,0:T(8,128)(2,1)}), bf16[32,64,1024]{2,1,0:T(8,128)(2,1)}, u32[]{:S(2)}, u32[]{:S(2)}) %all-to-all-start.1) | async-done | bytes 4194336 | tf_op jit(solution)/shard_map/all_to_all | solution.py:88
  192.1 7.4 %reshape.175 = bf16[64,32768]{1,0:T(8,128)(2,1)} reshape(bf16[32,64,1024]{2,1,0:T(8,128)(2,1)} %all-to-all-done.1) | data formatting | bytes 8388608 | tf_op jit(solution)/shard_map/reshape | solution.py:56
  199.5 4.9 fusion.36
  204.4 5.1 reshape.183
  209.5 6.1 %fusion.38 = (f32[]{:T(128)}, bf16[1024,1024]{1,0:T(8,128)(2,1)}, bf16[1024,1024]{1,0:T(8,128)(2,1)}) fusion(f32[1024,1024]{1,0:T(8,128)} %reshape.183, bf16[1024,1024]{1,0:T(8,128)(2,1)S(1)} %copy-done.1, f32[]{:T(128)} %bitcast.15), kind=kLoop, calls=%fused_computation.51 | loop fusion | flops 7340031 | bytes 10485768 | tf_op jit(solution)/shard_map/reduce_sum | solution.py:141
  215.6 2.9 reshape.176
  218.5 3.2 convolution_convert_fusion.1
  221.7 7.4 %reshape.177 = bf16[32,64,1024]{2,1,0:T(8,128)(2,1)} reshape(bf16[64,32768]{1,0:T(8,128)(2,1)} %convolution_convert_fusion.1) | data formatting | bytes 8388608 | tf_op jit(solution)/shard_map/reshape | solution.py:53
  229.1 8.0 %all-to-all-start.2 = ((bf16[32,64,1024]{2,1,0:T(8,128)(2,1)}), bf16[32,64,1024]{2,1,0:T(8,128)(2,1)}, u32[]{:S(2)}, u32[]{:S(2)}) async-start(bf16[32,64,1024]{2,1,0:T(8,128)(2,1)} %reshape.177), calls=%async_computation.2 | async-start | bytes 8388608 | tf_op jit(solution)/shard_map/all_to_all | solution.py:92
  237.1 50.2 %all-to-all-done.2 = bf16[32,64,1024]{2,1,0:T(8,128)(2,1)} async-done(((bf16[32,64,1024]{2,1,0:T(8,128)(2,1)}), bf16[32,64,1024]{2,1,0:T(8,128)(2,1)}, u32[]{:S(2)}, u32[]{:S(2)}) %all-to-all-start.2) | async-done | bytes 4194336 | tf_op jit(solution)/shard_map/all_to_all | solution.py:92
  287.3 102.2 %while.26 = (s32[]{:T(128)}, f32[768,1,128]{0,2,1:T(8,128)S(1)}, f32[768,1,128]{0,2,1:T(8,128)}, bf16[4,512,1024]{2,1,0:T(8,128)(2,1)}, bf16[4,512,1024]{1,2,0:T...) while((s32[]{:T(128)}, f32[768,1,128]{0,2,1:T(8,128)S(1)}, ...), condition=%wide.region_9.10_spmd.clone, body=%wide.region_5.9_spmd.clone.sunk | while | flops 4079865856 | bytes 101663000 | solution.py:131
  296.2 2.9 fusion.88
  299.1 2.9 fusion.91
  302.0 5.1 fusion.89
  308.2 3.1 convolution_convert_fusion.6
  321.8 2.9 fusion.88
  324.7 2.9 fusion.91
  327.7 5.1 fusion.89
  333.8 3.1 convolution_convert_fusion.6
  347.3 2.9 fusion.88
  350.2 2.9 fusion.91
  353.2 5.1 fusion.89
  359.3 3.1 convolution_convert_fusion.6
  372.9 2.9 fusion.88
  375.8 2.9 fusion.91
  378.7 5.1 fusion.89
  384.9 3.1 convolution_convert_fusion.6
  389.5 8.2 %all-to-all-start.3 = ((bf16[32,64,1024]{2,1,0:T(8,128)(2,1)}), bf16[32,64,1024]{2,1,0:T(8,128)(2,1)}, u32[]{:S(2)}, u32[]{:S(2)}) async-start(bf16[32,64,1024]{2,1,0:T(8,128)(2,1)} %bitcast.231), calls=%async_computation.3 | async-start | bytes 8388608 | tf_op jit(solution)/shard_map/all_to_all | solution.py:134
  397.7 106.5 %psum.7 = f32[]{:T(128)} all-reduce(f32[]{:T(128)} %get-tuple-element.180), channel_id=1, replica_groups=mesh['seq'=32,'mp'=4] {'seq','mp'}, use_global_device_ids=true, to_apply=%region_11.12 | all-reduce | flops 1 | bytes 8 | tf_op jit(solution)/shard_map/psum | solution.py:142
  506.5 7.4 %reshape.178 = bf16[64,32768]{1,0:T(8,128)(2,1)} reshape(bf16[32,64,1024]{2,1,0:T(8,128)(2,1)} %all-to-all-done.3) | data formatting | bytes 8388608 | tf_op jit(solution)/shard_map/reshape | solution.py:56
  513.9 2.9 convolution_convert_fusion.3
  (105 shorter events, 70.8 us)
Async XLA Ops:
  2.2 216.4 %copy-start.8 = (s32[32]{0:T(128)}, s32[32]{0:T(128)S(1)}, u32[]{:S(2)}) copy-start(s32[32]{0:T(128)S(1)} %convert_add_fusion) | copy-start | bytes 388
  15.7 9.6 %copy-start.5 = (bf16[1,768,128]{2,1,0:T(8,128)(2,1)S(1)}, bf16[1,768,128]{2,1,0:T(8,128)(2,1)}, u32[]{:S(2)}) copy-start(bf16[1,768,128]{2,1,0:T(8,128)(2,1)} %param.11) | copy-start | bytes 589828
  15.7 11.6 %copy-start.6 = (bf16[1,768,128]{2,1,0:T(8,128)(2,1)S(1)}, bf16[1,768,128]{2,1,0:T(8,128)(2,1)}, u32[]{:S(2)}) copy-start(bf16[1,768,128]{2,1,0:T(8,128)(2,1)} %param.12) | copy-start | bytes 589828
  15.7 59.9 %all-to-all-start = ((bf16[32,64,1024]{2,1,0:T(8,128)(2,1)}), bf16[32,64,1024]{2,1,0:T(8,128)(2,1)}, u32[]{:S(2)}, u32[]{:S(2)}) async-start(bf16[32,64,1024]{2,1,0:T(8,128)(2,1)} %reshape.174), calls=%async_computation | async-start | bytes 8388608 | tf_op jit(solution)/shard_map/all_to_all | solution.py:73
  133.7 58.3 %all-to-all-start.1 = ((bf16[32,64,1024]{2,1,0:T(8,128)(2,1)}), bf16[32,64,1024]{2,1,0:T(8,128)(2,1)}, u32[]{:S(2)}, u32[]{:S(2)}) async-start(bf16[32,64,1024]{2,1,0:T(8,128)(2,1)} %bitcast.230), calls=%async_computation.1 | async-start | bytes 8388608 | tf_op jit(solution)/shard_map/all_to_all | solution.py:88
  204.4 5.1 copy-start.1
  229.1 58.2 %all-to-all-start.2 = ((bf16[32,64,1024]{2,1,0:T(8,128)(2,1)}), bf16[32,64,1024]{2,1,0:T(8,128)(2,1)}, u32[]{:S(2)}, u32[]{:S(2)}) async-start(bf16[32,64,1024]{2,1,0:T(8,128)(2,1)} %reshape.177), calls=%async_computation.2 | async-start | bytes 8388608 | tf_op jit(solution)/shard_map/all_to_all | solution.py:92
  296.2 2.9 copy-start
  296.2 2.9 copy-start.2
  299.1 2.9 copy-start.7
  302.0 5.1 copy-start.3
  321.8 2.9 copy-start
  321.8 2.9 copy-start.2
  324.7 2.9 copy-start.7
  327.6 5.1 copy-start.3
  347.3 2.9 copy-start
  347.3 2.9 copy-start.2
  350.2 2.9 copy-start.7
  353.2 5.1 copy-start.3
  372.9 2.9 copy-start
  372.9 2.9 copy-start.2
  375.8 2.9 copy-start.7
  378.7 5.1 copy-start.3
  389.5 116.2 %copy-start.4 = (f32[768,1,128]{0,2,1:T(8,128)S(1)}, f32[768,1,128]{0,2,1:T(8,128)}, u32[]{:S(2)}) copy-start(f32[768,1,128]{0,2,1:T(8,128)} %get-tuple-element.84) | copy-start | bytes 1179652
  389.5 117.0 %all-to-all-start.3 = ((bf16[32,64,1024]{2,1,0:T(8,128)(2,1)}), bf16[32,64,1024]{2,1,0:T(8,128)(2,1)}, u32[]{:S(2)}, u32[]{:S(2)}) async-start(bf16[32,64,1024]{2,1,0:T(8,128)(2,1)} %bitcast.231), calls=%async_computation.3 | async-start | bytes 8388608 | tf_op jit(solution)/shard_map/all_to_all | solution.py:134
  506.5 7.4 %copy-start.9 = (s32[32]{0:T(128)S(1)}, s32[32]{0:T(128)}, u32[]{:S(2)}) copy-start(s32[32]{0:T(128)} %copy-done.8) | copy-start | bytes 388
where the time goes:
time: 523 us; the launch traced here: 520 us
  waiting for transfers between devices  148 us (28%)
  blocking collectives  107 us (20%)
  matrix products  99.1 us (19%)
  local copies, waits for them, and re-layouts  90.7 us (17%)
  other arithmetic  38.4 us (7%)
  starting transfers between devices  33.7 us (6%)
    psum x1, blocking collectives, body(): grand_total = lax.psum(partial_value, ('seq', 'mp'))  107 us
    all_to_all x1, waiting for transfers between devices, body(): lax.all_to_all(send_out(attn_grad), 'seq', split_axis=0, concat_axis=0, t...  50.2 us
    all_to_all x1, waiting for transfers between devices, body(): lax.all_to_all(output_rows.reshape(lane_shape), 'seq', split_axis=0, conc...  49.7 us
    all_to_all x1, waiting for transfers between devices, body(): lax.all_to_all(send_out(queries), 'seq', split_axis=0, concat_axis=0, til...  48.2 us
    reduce_sum x8, other arithmetic, softmax_rows(): return expo_terms / jnp.sum(expo_terms, axis=3, keepdims=True)  23.3 us
    dynamic_slice x16, local copies, waits for them, and re-layouts, body(): lax.map(attend_block, query_rows.reshape(block_count, block_rows, columns))  20.8 us
    dot_general x4, matrix products, grad_step(): jnp.einsum('bngd,knd->ngbk', grad_block, values_heads, preferred_element_...  20.2 us
    dot_general x8, matrix products, softmax_rows(): jnp.einsum('bngd,knd->ngbk', query_block, keys_heads, preferred_element_t...  19 us
  transfers between devices with their start and end apart: 4, of which 3 were waited for; matrix products, arithmetic and copies ran while one was open for 1% of the time, Pallas kernels for 0%

commit v1 on v0

v1 whole, which is shorter than its diff:
```python
import functools
import math

import jax
import jax.numpy as jnp
from jax import lax
from jax.experimental import pallas as pl
from jax.experimental.pallas import tpu as pltpu
from jax.sharding import PartitionSpec as P

HEAD = 128
RING = 4
MESH = pl.DeviceIdType.MESH
F32 = jnp.float32
BF16 = jnp.bfloat16


def nt(left, right):
    return lax.dot_general(left, right, (((1,), (1,)), ((), ())), preferred_element_type=F32)


def nn(left, right):
    return lax.dot_general(left, right, (((1,), (0,)), ((), ())), preferred_element_type=F32)


def tn(left, right):
    return lax.dot_general(left, right, (((0,), (0,)), ((), ())), preferred_element_type=F32)


def wrap(value):
    return lax.rem(value + RING, RING)


def kernel(
    sizes,
    tiles,
    slots,
    gate,
    q_hbm,
    k_hbm,
    v_hbm,
    c_hbm,
    att_hbm,
    dq_hbm,
    dk_hbm,
    dv_hbm,
    gate_out,
    kall,
    vall,
    probs,
    qv,
    cv,
    qs,
    gs,
    part,
    l3,
    lb1,
    lb2,
    la1,
    la2,
    l0,
    gacc,
    gland,
    send,
    recv,
    loc,
):
    spans, span_len, heads, image_len, total_elems = sizes
    scale = 1.0 / math.sqrt(HEAD)
    me = lax.axis_index("seq")
    my = lax.axis_index("mp")
    z = lax.div(me, 8)
    x = lax.rem(lax.div(me, 2), RING)
    c = lax.rem(me, 2)
    mate = me + 1 - 2 * c
    a = z * (1 - c) + x * c
    b = x * (1 - c) + z * c
    stride_a = 4 - 3 * c
    stride_b = 1 + 3 * c

    def pair(da, db):
        return wrap(a + da) * stride_a + wrap(b + db) * stride_b

    def mate_pair(da, db):
        return wrap(b + da) * stride_b + wrap(a + db) * stride_a

    def at(da, db):
        return (2 * pair(da, db) + c, my)

    barrier = pltpu.get_barrier_semaphore()
    friends = [(mate, my)]
    for d in range(1, RING):
        friends.append((8 * wrap(z + d) + 2 * x + c, my))
        friends.append((8 * z + 2 * wrap(x + d) + c, my))
        friends.append((me, wrap(my + d)))
    for friend in friends:
        pl.semaphore_signal(barrier, inc=1, device_id=friend, device_id_type=MESH)

    k_in = pltpu.make_async_copy(k_hbm, kall.at[pl.ds(me, 1)], loc.at[0])
    v_in = pltpu.make_async_copy(v_hbm, vall.at[pl.ds(me, 1)], loc.at[1])
    q_in = pltpu.make_async_copy(q_hbm, qv, loc.at[2])
    c_in = pltpu.make_async_copy(c_hbm, cv, loc.at[3])
    k_in.start()
    q_in.start()
    c_in.start()
    v_in.start()
    pl.semaphore_wait(barrier, len(friends))

    started = []

    def remote(src, dst, index, target):
        return pltpu.make_async_remote_copy(
            src_ref=src,
            dst_ref=dst,
            send_sem=send.at[index],
            recv_sem=recv.at[index],
            device_id=target,
            device_id_type=MESH,
        )

    def start(make):
        make().start()
        started.append(make)

    half = image_len // 2
    quarter = half // 2
    steps = (0, -1, 1, 2)

    def gather(buf, base):
        mine, other = c * half, (1 - c) * half

        def piece(which, first, rows):
            return buf.at[pl.ds(2 * which, 2), pl.ds(pl.multiple_of(first, 64), rows), :]

        def own_copy(first, tile, index):
            ref = buf.at[pl.ds(tile, 1), pl.ds(pl.multiple_of(first, 64), half), :]
            return remote(ref, ref, base + index, (mate, my))

        def moved(which, direction, index, target, narrow):
            if narrow:
                ref = piece(which, mine + direction * quarter, quarter)
            else:
                ref = piece(which, mine, half)
            return remote(ref, ref, base + index, target)

        def to_mate(k, kb):
            ref = piece(pair(steps[k], steps[kb]), mine, half)
            return remote(ref, ref, base + 24 + 4 * k + kb, (mate, my))

        def from_mate(k, kb):
            ref = piece(mate_pair(steps[k], steps[kb]), other, half)
            return remote(ref, ref, base + 24 + 4 * k + kb, (mate, my))

        sign = (1, -1)

        def e0():
            start(lambda: own_copy(other, me, 0))
            start(lambda: own_copy(mine, me, 1))

        def send_b(k):
            for d in range(2):
                start(lambda d=d: moved(pair(steps[k], 0), d, 8 + 4 * k + d, at(0, sign[d]), False))

        def e1():
            own_copy(mine, mate, 0).wait_recv()
            for d in range(2):
                start(lambda d=d: moved(pair(0, 0), d, 2 + d, at(sign[d], 0), False))
            send_b(0)

        def e_a(d):
            moved(pair(-sign[d], 0), d, 2 + d, at(sign[d], 0), False).wait_recv()
            start(lambda: moved(pair(-sign[d], 0), d, 4 + d, at(sign[d], 0), True))
            send_b(1 + d)
            start(lambda: to_mate(1 + d, 0))

        def e_aq():
            for d in range(2):
                moved(pair(2, 0), d, 4 + d, at(sign[d], 0), True).wait_recv()
            send_b(3)
            start(lambda: to_mate(3, 0))

        def e_b(k, d):
            moved(pair(steps[k], -sign[d]), d, 8 + 4 * k + d, at(0, sign[d]), False).wait_recv()
            start(
                lambda: moved(
                    pair(steps[k], -sign[d]), d, 10 + 4 * k + d, at(0, sign[d]), True
                )
            )
            start(lambda: to_mate(k, 1 + d))

        def e_bq(k):
            for d in range(2):
                moved(pair(steps[k], 2), d, 10 + 4 * k + d, at(0, sign[d]), True).wait_recv()
            start(lambda: to_mate(k, 3))

        def e_end():
            own_copy(other, mate, 1).wait_recv()
            for k in range(4):
                for kb in range(4):
                    if k or kb:
                        from_mate(k, kb).wait_recv()

        events = [
            lambda: e_a(0),
            lambda: e_a(1),
            lambda: e_b(0, 0),
            lambda: e_b(0, 1),
            e_aq,
            lambda: e_bq(0),
            lambda: e_b(1, 0),
            lambda: e_b(1, 1),
            lambda: e_b(2, 0),
            lambda: e_b(2, 1),
            lambda: e_bq(1),
            lambda: e_b(3, 0),
            lambda: e_b(3, 1),
            lambda: e_bq(2),
            lambda: e_bq(3),
        ]
        return e0, e1, events, e_end

    lane_half = HEAD // 2
    lane_quarter = HEAD // 4

    def reduce(y, base):
        mine, other = c * lane_half, (1 - c) * lane_half

        def piece(which, first, rows):
            return part.at[y, pl.ds(2 * which, 2), pl.ds(pl.multiple_of(first, 32), rows), :]

        def to_mate(which):
            return remote(piece(which, other, lane_half), l3.at[y, which], base + which, (mate, my))

        def add(which, first, rows, *landed):
            view = (y, pl.ds(2 * which, 2), pl.ds(pl.multiple_of(first, 32), rows), slice(None))
            total = part[view].astype(F32)
            for ref in landed:
                total = total + ref[...].astype(F32)
            part[view] = total.astype(BF16)

        def fold(which):
            to_mate(which).wait_recv()
            add(which, mine, lane_half, l3.at[y, which])

        def near(which, d, land, index, target, narrow):
            if narrow:
                ref = piece(which, mine + d * lane_quarter, lane_quarter)
            else:
                ref = piece(which, mine, lane_half)
            return remote(ref, land, base + index, target)

        sign = (-1, 1)

        def first_b(k, d):
            return near(pair(k, 2), d, lb1.at[y, k, d], 16 + 4 * k + d, at(0, sign[d]), True)

        def second_b(k, d):
            return near(pair(k, sign[d]), d, lb2.at[y, k, d], 18 + 4 * k + d, at(0, sign[d]), False)

        def first_a(d):
            return near(pair(2, 0), d, la1.at[y, d], 32 + d, at(sign[d], 0), True)

        def second_a(d):
            return near(pair(sign[d], 0), d, la2.at[y, d], 34 + d, at(sign[d], 0), False)

        def r1(k):
            fold(pair(k, 2))
            for d in range(2):
                start(lambda d=d: first_b(k, d))

        def r2(k):
            for d in range(2):
                fold(pair(k, sign[d]))
                first_b(k, d).wait_recv()
                add(pair(k, sign[d]), mine + d * lane_quarter, lane_quarter, lb1.at[y, k, d])
                start(lambda d=d: second_b(k, d))

        def r3(k):
            fold(pair(k, 0))
            for d in range(2):
                second_b(k, d).wait_recv()
            add(pair(k, 0), mine, lane_half, lb2.at[y, k, 0], lb2.at[y, k, 1])
            if k == 2:
                for d in range(2):
                    start(lambda d=d: first_a(d))
            if k in (1, 3):
                d = 0 if k == 3 else 1
                first_a(d).wait_recv()
                add(pair(sign[d], 0), mine + d * lane_quarter, lane_quarter, la1.at[y, d])
                start(lambda: second_a(d))

        def last():
            def make(first, tile):
                ref = part.at[y, tile, pl.ds(pl.multiple_of(first, 32), lane_half), :]
                return remote(ref, l0.at[y], base + 36, (mate, my))

            for d in range(2):
                second_a(d).wait_recv()
            add(pair(0, 0), mine, lane_half, la2.at[y, 0], la2.at[y, 1])
            start(lambda: make(mine, mate))
            make(mine, mate).wait_recv()

        order = (2, 3, 1, 0)
        events = [functools.partial(r1, k) for k in order]
        events += [functools.partial(r2, k) for k in order]
        events += [functools.partial(r3, k) for k in order]
        return to_mate, events, last

    def outs(y, hbm, index):
        mine, other = c * lane_half, (1 - c) * lane_half
        near_out = pltpu.make_async_copy(
            part.at[y, me, pl.ds(pl.multiple_of(mine, 32), lane_half), :],
            hbm.at[pl.ds(pl.multiple_of(mine, 32), lane_half), :],
            loc.at[index],
        )
        far_out = pltpu.make_async_copy(
            l0.at[y], hbm.at[pl.ds(pl.multiple_of(other, 32), lane_half), :], loc.at[index + 1]
        )
        return near_out, far_out

    k0, k1, k_events, k_end = gather(kall, 0)
    v0, v1, v_events, v_end = gather(vall, 40)
    v_mate, dv_events, dv_last = reduce(0, 80)
    k_mate, dk_events, dk_last = reduce(1, 120)

    def scheduled(step, table):
        for moment, event in table:
            pl.when(step == moment)(event)

    k_in.wait()
    k0()
    gate_tanh = jnp.tanh(jnp.full((8, HEAD), gate[0], F32))
    tanh_row = jnp.broadcast_to(gate_tanh[0:1, 0:1], (span_len, HEAD))
    gacc[...] = jnp.zeros((8, HEAD), F32)
    k1()
    q_in.wait()
    c_in.wait()
    qs[spans] = jnp.zeros((heads * span_len, HEAD), BF16)
    gs[spans] = jnp.zeros((heads * span_len, HEAD), BF16)

    def lay_out(s, carry):
        rows = pl.ds(pl.multiple_of(s * span_len, span_len), span_len)
        for h in range(heads):
            cols = slice(h * HEAD, (h + 1) * HEAD)
            qs[s, h * span_len : (h + 1) * span_len, :] = qv[rows, cols]
            gs[s, h * span_len : (h + 1) * span_len, :] = (
                tanh_row * cv[rows, cols].astype(F32)
            ).astype(BF16)
        return carry

    lax.fori_loop(0, spans, lay_out, 0)
    v_in.wait()
    for event in k_events:
        event()
    v0()
    k_end()
    v1()

    def soften(s, carry):
        scores = nt(qs[s], kall[tiles[s]])
        top = jnp.max(scores, axis=1, keepdims=True)
        expo = jnp.exp((scores - top) * scale)
        inv = 1.0 / jnp.sum(expo, axis=1, keepdims=True)
        probs[s] = (expo * inv).astype(BF16)
        scheduled(s, zip((8, 10, 12, 13, 18, 20, 23, 25, 28, 30), v_events[:10]))
        return carry

    lax.fori_loop(0, spans, soften, 0)

    def tile_sum(rows, weights, tile):
        s0, s1 = slots[0, tile], slots[1, tile]
        cap = spans - 1
        return tn(rows[s0], weights[jnp.minimum(s0, cap)]) + tn(
            rows[s1], weights[jnp.minimum(s1, cap)]
        )

    def value_part(p, carry):
        for i in range(2):
            part[0, 2 * p + i] = tile_sum(gs, probs, 2 * p + i).astype(BF16)
        v_mate(p).start()
        scheduled(p, zip((1, 4, 6, 9, 12), v_events[10:]))
        return carry

    lax.fori_loop(0, spans // 2, value_part, 0)
    v_end()

    def backward(s, carry):
        rows = pl.ds(pl.multiple_of(s * span_len, span_len), span_len)
        values, weights, grads = vall[tiles[s]], probs[s], gs[s]
        attn = nn(weights, values).astype(BF16)
        attn_f = attn.astype(F32)
        delta = jnp.sum(grads.astype(F32) * attn_f, axis=1, keepdims=True)
        dscore = (weights.astype(F32) * (nt(grads, values) - delta) * scale).astype(BF16)
        probs[s] = dscore
        dq = nn(dscore, kall[tiles[s]]).astype(BF16)
        total = jnp.zeros((span_len, HEAD), F32)
        for h in range(heads):
            cols = slice(h * HEAD, (h + 1) * HEAD)
            block = slice(h * span_len, (h + 1) * span_len)
            qv[rows, cols] = dq[block]
            total = total + cv[rows, cols].astype(F32) * attn_f[block]
            cv[rows, cols] = (tanh_row * attn_f[block]).astype(BF16)
        gacc[...] += sum(total[8 * i : 8 * i + 8] for i in range(span_len // 8))
        scheduled(s, zip((0, 1, 2, 3, 14, 18, 22, 26), dv_events[:8]))
        return carry

    lax.fori_loop(0, spans, backward, 0)
    att_out = pltpu.make_async_copy(cv, att_hbm, loc.at[4])
    dq_out = pltpu.make_async_copy(qv, dq_hbm, loc.at[5])
    att_out.start()
    dq_out.start()

    def key_part(p, carry):
        for i in range(2):
            part[1, 2 * p + i] = tile_sum(qs, probs, 2 * p + i).astype(BF16)
        k_mate(p).start()
        scheduled(p, zip((2, 5, 8, 12), dv_events[8:]))
        return carry

    lax.fori_loop(0, spans // 2, key_part, 0)

    def exchange(stage, own, count, targets, base):
        for d, target in enumerate(targets):
            start(
                lambda d=d, target=target: remote(
                    gland.at[stage, own], gland.at[stage, own], base + d, target
                )
            )

    def settle(stage, count, targets, base):
        for d, target in enumerate(targets):
            remote(gland.at[stage, 0], gland.at[stage, 0], base + d, target).wait_recv()
        total = gland[stage, 0]
        for i in range(1, count):
            total = total + gland[stage, i]
        return total

    rings = (
        (c, 2, [(mate, my)]),
        (z, RING, [(8 * wrap(z + d) + 2 * x + c, my) for d in range(1, RING)]),
        (x, RING, [(8 * z + 2 * wrap(x + d) + c, my) for d in range(1, RING)]),
        (my, RING, [(me, wrap(my + d)) for d in range(1, RING)]),
    )
    gate_base = 160

    def gate_begin(stage, value):
        own, count, targets = rings[stage]
        gland[stage, own] = value
        exchange(stage, own, count, targets, gate_base + 3 * stage)

    def gate_end(stage):
        own, count, targets = rings[stage]
        return settle(stage, count, targets, gate_base + 3 * stage)

    gate_begin(0, gacc[...])
    for event in dk_events[:4]:
        event()
    dv_last()
    dv_outs = outs(0, dv_hbm, 6)
    for copy in dv_outs:
        copy.start()
    for event in dk_events[4:8]:
        event()
    gate_begin(1, gate_end(0))
    dk_events[8]()
    gate_begin(2, gate_end(1))
    dk_events[9]()
    dk_events[10]()
    gate_begin(3, gate_end(2))
    dk_events[11]()
    dk_last()
    dk_outs = outs(1, dk_hbm, 8)
    for copy in dk_outs:
        copy.start()
    grand = jnp.sum(gate_end(3))
    slope = (1.0 - gate_tanh * gate_tanh) * grand / math.sqrt(total_elems)
    gate_out[...] = slope

    for make in started:
        make().wait_send()

    def drain(p, carry):
        v_mate(p).wait_send()
        k_mate(p).wait_send()
        return carry

    lax.fori_loop(0, spans // 2, drain, 0)
    for copy in (att_out, dq_out) + dv_outs + dk_outs:
        copy.wait()


def body(queries, image_keys, image_values, span_tiles, gate_logit, cotangent):
    tok_count, columns = queries.shape
    spans = span_tiles.shape[0]
    span_len = tok_count // spans
    heads = columns // HEAD
    image_len = image_keys.shape[1]
    tile_count = lax.axis_size("seq")
    total_elems = tok_count * tile_count * columns * lax.axis_size("mp")
    owners = span_tiles[:, 0]
    numbers = jnp.arange(spans, dtype=jnp.int32)[:, None]
    hits = owners[:, None] == jnp.arange(tile_count, dtype=jnp.int32)[None, :]
    first = jnp.min(jnp.where(hits, numbers, spans), axis=0)
    final = jnp.max(jnp.where(hits, numbers, -1), axis=0)
    slots = jnp.stack([first, jnp.where(final > first, final, spans)])
    smem = pl.BlockSpec(memory_space=pltpu.SMEM)
    hbm = pl.BlockSpec(memory_space=pl.ANY)
    sizes = (spans, span_len, heads, image_len, total_elems)
    rows = heads * span_len
    kv = (tile_count, image_len, HEAD)
    att, dq, dk, dv, gate = pl.pallas_call(
        functools.partial(kernel, sizes),
        out_shape=(
            jax.ShapeDtypeStruct(queries.shape, BF16),
            jax.ShapeDtypeStruct(queries.shape, BF16),
            jax.ShapeDtypeStruct((HEAD, image_len), BF16),
            jax.ShapeDtypeStruct((HEAD, image_len), BF16),
            jax.ShapeDtypeStruct((8, HEAD), F32),
        ),
        in_specs=[smem, smem, smem, hbm, hbm, hbm, hbm],
        out_specs=(hbm, hbm, hbm, hbm, pl.BlockSpec(memory_space=pltpu.VMEM)),
        scratch_shapes=[
            pltpu.VMEM(kv, BF16),
            pltpu.VMEM(kv, BF16),
            pltpu.VMEM((spans, rows, image_len), BF16),
            pltpu.VMEM(queries.shape, BF16),
            pltpu.VMEM(queries.shape, BF16),
            pltpu.VMEM((spans + 1, rows, HEAD), BF16),
            pltpu.VMEM((spans + 1, rows, HEAD), BF16),
            pltpu.VMEM((2, tile_count, HEAD, image_len), BF16),
            pltpu.VMEM((2, tile_count // 2, 2, HEAD // 2, image_len), BF16),
            pltpu.VMEM((2, RING, 2, 2, HEAD // 4, image_len), BF16),
            pltpu.VMEM((2, RING, 2, 2, HEAD // 2, image_len), BF16),
            pltpu.VMEM((2, 2, 2, HEAD // 4, image_len), BF16),
            pltpu.VMEM((2, 2, 2, HEAD // 2, image_len), BF16),
            pltpu.VMEM((2, HEAD // 2, image_len), BF16),
            pltpu.VMEM((8, HEAD), F32),
            pltpu.VMEM((4, RING, 8, HEAD), F32),
            pltpu.SemaphoreType.DMA((172,)),
            pltpu.SemaphoreType.DMA((172,)),
            pltpu.SemaphoreType.DMA((10,)),
        ],
        compiler_params=pltpu.CompilerParams(
            collective_id=0, has_side_effects=True, vmem_limit_bytes=67043328
        ),
        name="cross_attention",
    )(owners, slots, gate_logit, queries, image_keys, image_values, cotangent)
    return (att, dq, dk.T[None], dv.T[None], gate[0, :1])


def solution(mesh):
    placed = (
        P("seq", "mp"),
        P("seq", None, "mp"),
        P("seq", None, "mp"),
        P("seq", None),
        P(),
        P("seq", "mp"),
    )
    return jax.shard_map(
        body,
        mesh=mesh,
        in_specs=placed,
        out_specs=(P("seq", "mp"), P("seq", "mp"), P("seq", None, "mp"), P("seq", None, "mp"), P()),
        check_vma=False,
    )
```

time: 523 us -> 134 us (0.26)
  waiting for transfers between devices: 148 us -> 0 us
  Pallas kernels: 0 us -> 122 us
  blocking collectives: 107 us -> 0 us
  matrix products: 99.1 us -> 0 us
  local copies, waits for them, and re-layouts: 90.7 us -> 9.22 us
  other arithmetic: 38.4 us -> 1.32 us
  starting transfers between devices: 33.7 us -> 0 us
    all_to_all x4 -> x0, waiting for transfers between devices: 148 us -> none  [the longest x1 50.2 us: body(): lax.all_to_all(send_out(attn_grad), 'seq', split_axis=0, concat_axis=0, t...]
    pallas_call x0 -> x1, Pallas kernels: none -> 122 us  [body(): pl.pallas_call(functools.partial(kernel, sizes), out_shape=(jax.ShapeDtyp...]
    psum x1 -> x0, blocking collectives: 107 us -> none  [body(): grand_total = lax.psum(partial_value, ('seq', 'mp'))]
    dot_general x33 -> x0, matrix products: 99.1 us -> none  [the longest x4 20.2 us: grad_step(): jnp.einsum('bngd,knd->ngbk', grad_block, values_heads, preferred_element_...]
    reshape x7 -> x0, local copies, waits for them, and re-layouts: 37.7 us -> none  [the longest x2 14.8 us: bring_home(): flat_rows = packed.reshape(slot_count, span_len * columns)]
    all_to_all x4 -> x0, starting transfers between devices: 33.7 us -> none  [the longest x1 9.62 us: body(): lax.all_to_all(send_out(queries), 'seq', split_axis=0, concat_axis=0, til...]
    reduce_sum x13 -> x0, other arithmetic: 30.4 us -> none  [the longest x8 23.3 us: softmax_rows(): return expo_terms / jnp.sum(expo_terms, axis=3, keepdims=True)]
    dynamic_slice x16 -> x0, local copies, waits for them, and re-layouts: 20.8 us -> none  [body(): lax.map(attend_block, query_rows.reshape(block_count, block_rows, columns))]
  transfers between devices with their start and end apart: 4 -> 0, of which waited for: 3 -> 0; matrix products, arithmetic and copies ran while one was open for 1% -> 0% of each run, Pallas kernels for 0% -> 0%
where the time goes in v1:
time: 134 us
  Pallas kernels  122 us (91%)
  local copies, waits for them, and re-layouts  9.22 us (7%)
    pallas_call x1, Pallas kernels, body(): pl.pallas_call(functools.partial(kernel, sizes), out_shape=(jax.ShapeDtyp...  122 us
    unnamed x6, local copies, waits for them, and re-layouts  8.03 us

profile of v1, /device:TPU:1, one launch (start us, length us, event | category | flops | bytes accessed | tf_op | source)
XLA Modules:
  0.0 134.0 jit_solution(1136659431179249270)
XLA Ops:
  1.3 0.7 select_reduce_fusion.1
  2.0 0.6 pad_add_fusion.slots
  2.6 122.2 %cross_attention.1 = (bf16[1024,1024]{1,0:T(8,128)(2,1)}, bf16[1024,1024]{1,0:T(8,128)(2,1)}, bf16[128,768]{1,0:T(8,128)(2,1)}, bf16[128,768]{1,0:T(8,128)(2,1)}, f32[8,128]{1,0:T(8,128)}) custom-call(s32[32]{0:T(128)} %bitcast.15, s32[2,32]{1,0:T(2,128)} %pad_add_fusion.slots, f32[1]{0:T(128)S(6)} %copy.17.gate, bf16[1024,1024]{1,0:T(8,128)(2,1)} %q_hbm.1, ...), custom_call_target="tpu_custom_call" | custom-call | tf_op jit(solution)/shard_map/cross_attention/pallas_call | solution.py:511
  124.8 1.2 slice.3
  126.0 1.7 %copy.13 = bf16[1,768,128]{2,1,0:T(8,128)(2,1)} copy(bf16[1,768,128]{1,2,0:T(8,128)(2,1)} %bitcast.13) | data formatting | bytes 393216
  127.7 1.7 %copy.14 = bf16[1,768,128]{2,1,0:T(8,128)(2,1)} copy(bf16[1,768,128]{1,2,0:T(8,128)(2,1)} %bitcast.12) | data formatting | bytes 393216
  129.5 0.0 copy-start
  129.5 3.2 %copy.18 = bf16[1024,1024]{1,0:T(8,128)(2,1)} copy(bf16[1024,1024]{1,0:T(8,128)(2,1)} %get-tuple-element.32) | data formatting | bytes 4194304
  132.7 0.0 copy-done
  132.7 1.3 copy.19
  (1 shorter events, 0.0 us)
Async XLA Ops:
  129.5 3.2 %copy-start = (bf16[1024,1024]{1,0:T(8,128)(2,1)S(1)}, bf16[1024,1024]{1,0:T(8,128)(2,1)}, u32[]{:S(2)}) copy-start(bf16[1024,1024]{1,0:T(8,128)(2,1)} %get-tuple-element.33) | copy-start | bytes 6291460

commit v2 on v1

v2 whole, which is shorter than its diff:
```python
import functools
import math

import jax
import jax.numpy as jnp
from jax import lax
from jax.experimental import pallas as pl
from jax.experimental.pallas import tpu as pltpu
from jax.sharding import PartitionSpec as P

HEAD = 128
RING = 4
LOG2E = 1.4426950408889634
MESH = pl.DeviceIdType.MESH
F32 = jnp.float32
BF16 = jnp.bfloat16


def nt(left, right):
    return lax.dot_general(left, right, (((1,), (1,)), ((), ())), preferred_element_type=F32)


def nn(left, right):
    return lax.dot_general(left, right, (((1,), (0,)), ((), ())), preferred_element_type=F32)


def tn(left, right):
    return lax.dot_general(left, right, (((0,), (0,)), ((), ())), preferred_element_type=F32)


def wrap(value):
    return lax.rem(value + RING, RING)


def kernel(
    sizes,
    tiles,
    gate,
    q_hbm,
    k_hbm,
    v_hbm,
    c_hbm,
    att_hbm,
    dq_hbm,
    dk_hbm,
    dv_hbm,
    gate_out,
    kall,
    vall,
    probs,
    cs,
    qs,
    gs,
    alone,
    part,
    slots_v,
    slots,
    l3,
    lb1,
    lb2,
    la1,
    la2,
    l0,
    upright,
    wide_a,
    wide_b,
    thin_a,
    thin_b,
    mid_a,
    mid_b,
    gacc,
    gland,
    send,
    recv,
    loc,
    free,
):
    spans, span_len, heads, image_len, total_elems = sizes
    scale = 1.0 / math.sqrt(HEAD)
    me = lax.axis_index("seq")
    my = lax.axis_index("mp")
    z = lax.div(me, 8)
    x = lax.rem(lax.div(me, 2), RING)
    c = lax.rem(me, 2)
    mate = me + 1 - 2 * c
    a = z * (1 - c) + x * c
    b = x * (1 - c) + z * c
    stride_a = 4 - 3 * c
    stride_b = 1 + 3 * c

    def pair(da, db):
        return wrap(a + da) * stride_a + wrap(b + db) * stride_b

    def mate_pair(da, db):
        return wrap(b + da) * stride_b + wrap(a + db) * stride_a

    def at(da, db):
        return (2 * pair(da, db) + c, my)

    barrier = pltpu.get_barrier_semaphore()
    friends = [(mate, my)]
    for d in range(1, RING):
        friends.append((8 * wrap(z + d) + 2 * x + c, my))
        friends.append((8 * z + 2 * wrap(x + d) + c, my))
        friends.append((me, wrap(my + d)))
    for friend in friends:
        pl.semaphore_signal(barrier, inc=1, device_id=friend, device_id_type=MESH)

    def by_head(hbm, buf, index, out):
        copies = []
        for h in range(heads):
            flat_side = hbm.at[:, :, pl.ds(h * HEAD, HEAD)]
            head_side = buf.at[pl.ds(0, spans), pl.ds(h * span_len, span_len), :]
            src, dst = (head_side, flat_side) if out else (flat_side, head_side)
            copies.append(pltpu.make_async_copy(src, dst, loc.at[index + h]))
        return copies

    k_in = pltpu.make_async_copy(k_hbm, kall.at[pl.ds(me, 1)], loc.at[0])
    v_in = pltpu.make_async_copy(v_hbm, vall.at[pl.ds(me, 1)], loc.at[1])
    rows_in = by_head(q_hbm, qs, 4, False) + by_head(c_hbm, cs, 4 + heads, False)
    k_in.start()
    v_in.start()
    for copy in rows_in:
        copy.start()
    pl.semaphore_wait(barrier, len(friends))

    started = []

    def remote(src, dst, index, target):
        return pltpu.make_async_remote_copy(
            src_ref=src,
            dst_ref=dst,
            send_sem=send.at[index],
            recv_sem=recv.at[index],
            device_id=target,
            device_id_type=MESH,
        )

    def start(make):
        make().start()
        started.append(make)

    half = image_len // 2
    quarter = half // 2
    steps = (0, -1, 1, 2)

    def gather(buf, base):
        mine, other = c * half, (1 - c) * half

        def piece(which, first, rows):
            return buf.at[pl.ds(2 * which, 2), pl.ds(pl.multiple_of(first, 64), rows), :]

        def own_copy(first, tile, index):
            ref = buf.at[pl.ds(tile, 1), pl.ds(pl.multiple_of(first, 64), half), :]
            return remote(ref, ref, base + index, (mate, my))

        def moved(which, direction, index, target, narrow):
            if narrow:
                ref = piece(which, mine + direction * quarter, quarter)
            else:
                ref = piece(which, mine, half)
            return remote(ref, ref, base + index, target)

        def to_mate(k, kb):
            ref = piece(pair(steps[k], steps[kb]), mine, half)
            return remote(ref, ref, base + 24 + 4 * k + kb, (mate, my))

        def from_mate(k, kb):
            ref = piece(mate_pair(steps[k], steps[kb]), other, half)
            return remote(ref, ref, base + 24 + 4 * k + kb, (mate, my))

        sign = (1, -1)

        def lone(tile, index, target):
            ref = buf.at[pl.ds(tile, 1), pl.ds(pl.multiple_of(mine, 64), half), :]
            return remote(ref, ref, base + index, target)

        def lone_a(tile, d, second):
            return lone(tile, (40 if second else 2) + d, at(sign[d], 0))

        def lone_b(tile, d, second):
            return lone(tile, (42 if second else 8) + d, at(0, sign[d]))

        def e0():
            start(lambda: own_copy(other, me, 0))
            for d in range(2):
                start(lambda d=d: lone_a(me, d, False))
                start(lambda d=d: lone_b(me, d, False))
            start(lambda: own_copy(mine, me, 1))

        def send_b(k):
            for d in range(2):
                start(lambda d=d: moved(pair(steps[k], 0), d, 8 + 4 * k + d, at(0, sign[d]), False))

        def e1():
            own_copy(mine, mate, 0).wait_recv()
            for d in range(2):
                start(lambda d=d: lone_a(mate, d, True))
                start(lambda d=d: lone_b(mate, d, True))

        def e_a(d):
            lone_a(2 * pair(-sign[d], 0) + c, d, False).wait_recv()
            lone_a(2 * pair(-sign[d], 0) + 1 - c, d, True).wait_recv()
            start(lambda: moved(pair(-sign[d], 0), d, 4 + d, at(sign[d], 0), True))
            send_b(1 + d)
            start(lambda: to_mate(1 + d, 0))

        def e_aq():
            for d in range(2):
                moved(pair(2, 0), d, 4 + d, at(sign[d], 0), True).wait_recv()
            send_b(3)
            start(lambda: to_mate(3, 0))

        def e_b(k, d):
            if k == 0:
                lone_b(2 * pair(0, -sign[d]) + c, d, False).wait_recv()
                lone_b(2 * pair(0, -sign[d]) + 1 - c, d, True).wait_recv()
            else:
                moved(pair(steps[k], -sign[d]), d, 8 + 4 * k + d, at(0, sign[d]), False).wait_recv()
            start(
                lambda: moved(
                    pair(steps[k], -sign[d]), d, 10 + 4 * k + d, at(0, sign[d]), True
                )
            )
            start(lambda: to_mate(k, 1 + d))

        def e_bq(k):
            for d in range(2):
                moved(pair(steps[k], 2), d, 10 + 4 * k + d, at(0, sign[d]), True).wait_recv()
            start(lambda: to_mate(k, 3))

        def e_end():
            own_copy(other, mate, 1).wait_recv()
            for k in range(4):
                for kb in range(4):
                    if k or kb:
                        from_mate(k, kb).wait_recv()

        events = [
            lambda: e_a(0),
            lambda: e_a(1),
            lambda: e_b(0, 0),
            lambda: e_b(0, 1),
            e_aq,
            lambda: e_b(1, 0),
            lambda: e_b(1, 1),
            lambda: e_b(2, 0),
            lambda: e_b(2, 1),
            lambda: e_bq(0),
            lambda: e_b(3, 0),
            lambda: e_b(3, 1),
            lambda: e_bq(1),
            lambda: e_bq(2),
            lambda: e_bq(3),
        ]
        return e0, e1, events, e_end

    lane_half = HEAD // 2
    lane_quarter = HEAD // 4

    def reduce(y, base):
        mine, other = c * lane_half, (1 - c) * lane_half

        def piece(which, first, rows):
            return part.at[y, pl.ds(2 * which, 2), pl.ds(pl.multiple_of(first, 32), rows), :]

        def landing(which):
            if y == 0:
                return l3.at[which]
            return probs.at[pl.ds(2 * which, 2), pl.ds(0, lane_half), :]

        def to_mate(which):
            return remote(piece(which, other, lane_half), landing(which), base + which, (mate, my))

        def add(which, first, rows, *landed):
            view = (y, pl.ds(2 * which, 2), pl.ds(pl.multiple_of(first, 32), rows), slice(None))
            total = part[view].astype(F32)
            for ref in landed:
                total = total + ref[...].astype(F32)
            part[view] = total.astype(BF16)

        def fold(which):
            to_mate(which).wait_recv()
            add(which, mine, lane_half, landing(which))

        def near(which, d, land, index, target, narrow):
            if narrow:
                ref = piece(which, mine + d * lane_quarter, lane_quarter)
            else:
                ref = piece(which, mine, lane_half)
            return remote(ref, land, base + index, target)

        sign = (-1, 1)

        def first_b(k, d):
            return near(pair(k, 2), d, lb1.at[y, k, d], 16 + 4 * k + d, at(0, sign[d]), True)

        def second_b(k, d):
            return near(pair(k, sign[d]), d, lb2.at[y, k, d], 18 + 4 * k + d, at(0, sign[d]), False)

        def first_a(d):
            return near(pair(2, 0), d, la1.at[y, d], 32 + d, at(sign[d], 0), True)

        def second_a(d):
            return near(pair(sign[d], 0), d, la2.at[y, d], 34 + d, at(sign[d], 0), False)

        def r1(k):
            fold(pair(k, 2))
            for d in range(2):
                start(lambda d=d: first_b(k, d))

        def r2(k):
            for d in range(2):
                fold(pair(k, sign[d]))
                first_b(k, d).wait_recv()
                add(pair(k, sign[d]), mine + d * lane_quarter, lane_quarter, lb1.at[y, k, d])
                start(lambda d=d: second_b(k, d))

        def r3(k):
            fold(pair(k, 0))
            for d in range(2):
                second_b(k, d).wait_recv()
            add(pair(k, 0), mine, lane_half, lb2.at[y, k, 0], lb2.at[y, k, 1])
            if k == 2:
                for d in range(2):
                    start(lambda d=d: first_a(d))
            if k in (1, 3):
                d = 0 if k == 3 else 1
                first_a(d).wait_recv()
                add(pair(sign[d], 0), mine + d * lane_quarter, lane_quarter, la1.at[y, d])
                start(lambda: second_a(d))

        def last():
            def make(first, tile):
                ref = part.at[y, tile, pl.ds(pl.multiple_of(first, 32), lane_half), :]
                return remote(ref, l0.at[y], base + 36, (mate, my))

            for d in range(2):
                second_a(d).wait_recv()
            add(pair(0, 0), mine, lane_half, la2.at[y, 0], la2.at[y, 1])
            start(lambda: make(mine, mate))
            make(mine, mate).wait_recv()

        order = (2, 3, 1, 0)
        events = [functools.partial(r1, k) for k in order]
        events += [functools.partial(r2, k) for k in order]
        events += [functools.partial(r3, k) for k in order]
        return to_mate, events, last

    def finish(y, hbm, index):
        mine, other = c * lane_half, (1 - c) * lane_half
        mid_a[pl.ds(pl.multiple_of(mine, 32), lane_half), :] = part[
            y, me, pl.ds(pl.multiple_of(mine, 32), lane_half), :
        ]
        mid_a[pl.ds(pl.multiple_of(other, 32), lane_half), :] = l0[y]
        upright[y] = mid_a[0:HEAD, :].T
        copy = pltpu.make_async_copy(upright.at[pl.ds(y, 1)], hbm, loc.at[index])
        copy.start()
        return copy

    k0, k1, k_events, k_end = gather(kall, 0)
    v0, v1, v_events, v_end = gather(vall, 44)
    v_mate, dv_events, dv_last = reduce(0, 88)
    k_mate, dk_events, dk_last = reduce(1, 128)

    def run(step, total, cuts):
        low = 0
        for high, events in cuts:
            if high > low:
                lax.fori_loop(low, high, step, 0)
            low = high
            for event in events:
                event()
        if low < total:
            lax.fori_loop(low, total, step, 0)

    def flush():
        for make in started:
            make().wait_send()
        started.clear()

    rings = (
        (c, [(mate, my)]),
        (z, [(8 * wrap(z + d) + 2 * x + c, my) for d in range(1, RING)]),
        (x, [(8 * z + 2 * wrap(x + d) + c, my) for d in range(1, RING)]),
        (my, [(me, wrap(my + d)) for d in range(1, RING)]),
    )
    gate_base = 168

    def gate_copy(stage, d):
        own, targets = rings[stage]
        ref = gland.at[stage, own]
        return remote(ref, ref, gate_base + 3 * stage + d, targets[d])

    def gate_begin(stage, value):
        own, targets = rings[stage]
        gland[stage, own] = value
        for d in range(len(targets)):
            start(lambda d=d: gate_copy(stage, d))

    def gate_end(stage):
        own, targets = rings[stage]
        for d in range(len(targets)):
            gate_copy(stage, d).wait_recv()
        total = gland[stage, 0]
        for i in range(1, len(targets) + 1):
            total = total + gland[stage, i]
        return total

    k_in.wait()
    k0()
    lane = lax.broadcasted_iota(jnp.int32, (1, HEAD), 1)
    first = final = jnp.full((1, HEAD), spans, jnp.int32)
    for s in range(spans):
        hit = lane == tiles[s]
        final = jnp.where(hit, s, final)
        first = jnp.where(hit & (first == spans), s, first)
    slots_v[0:1, :] = first
    slots_v[1:2, :] = jnp.where(final > first, final, spans)
    slots_copy = pltpu.make_async_copy(slots_v, slots, loc.at[2])
    slots_copy.start()
    gate_tanh = jnp.tanh(jnp.full((8, HEAD), gate[0], F32))
    tanh_row = jnp.broadcast_to(gate_tanh[0:1, 0:1], (heads * span_len, HEAD))
    gacc[...] = jnp.zeros((8, HEAD), F32)
    alone[spans] = jnp.zeros((HEAD, image_len), BF16)
    qs[spans] = jnp.zeros((heads * span_len, HEAD), BF16)
    mid_b[...] = jnp.zeros((heads * span_len, image_len), BF16)
    k1()
    v_in.wait()
    v0()
    for event in k_events[:9]:
        event()
    for copy in rows_in:
        copy.wait()

    def gated(s, carry):
        gs[s] = (tanh_row * cs[s].astype(F32)).astype(BF16)
        return carry

    lax.fori_loop(0, spans, gated, 0)
    for event in k_events[9:12]:
        event()
    v1()
    for event in k_events[12:]:
        event()
    k_end()

    cap = spans - 1

    def score(s, wide):
        wide[...] = nt(qs[s], kall[tiles[s]])

    def soften(s, wide, mid):
        scores = wide[...]
        top = jnp.max(scores, axis=1, keepdims=True)
        expo = jnp.exp2((scores - top) * (scale * LOG2E))
        inv = 1.0 / jnp.sum(expo, axis=1, keepdims=True)
        weights = (expo * inv).astype(BF16)
        probs[s] = weights
        mid[...] = weights

    def before(i):
        return jnp.where(i == 0, spans, 2 * i - 1)

    def value_alone(s, mid):
        alone[s] = tn(gs[jnp.minimum(s, cap)], mid[...]).astype(BF16)

    def soften_two(i, carry):
        score(2 * i + 1, wide_b)
        value_alone(before(i), mid_b)
        soften(2 * i, wide_a, mid_a)
        score(jnp.minimum(2 * i + 2, cap), wide_a)
        value_alone(2 * i, mid_a)
        soften(2 * i + 1, wide_b, mid_b)
        return carry

    score(0, wide_a)
    run(
        soften_two,
        spans // 2,
        (
            (4, v_events[:4]),
            (9, v_events[4:5]),
            (13, v_events[5:9]),
            (16, v_events[9:10]),
        ),
    )

    value_alone(cap, mid_b)
    mid_b[...] = jnp.zeros((heads * span_len, image_len), BF16)

    slots_copy.wait()

    def partials(y, mate_copy, cuts):
        def add_pair(which):
            for i in range(2):
                tile = 2 * which + i
                both = alone[slots[0, tile]].astype(F32) + alone[slots[1, tile]].astype(F32)
                part[y, tile] = both.astype(BF16)
            mate_copy(which).start()

        def along_x(i, carry):
            add_pair(RING * wrap(z + 2) + wrap(x + i))
            return carry

        def along_z(i, carry):
            add_pair(RING * wrap(z + 3 + i) + wrap(x + 2))
            return carry

        def inner(u):
            def step(i, carry):
                add_pair(RING * wrap(z + u) + wrap(x + 3 + i))
                return carry

            return step

        loops = [(along_x, 4), (along_z, 3), (inner(3), 3), (inner(1), 3), (inner(0), 3)]
        for (step, count), events in zip(loops, cuts):
            lax.fori_loop(0, count, step, 0)
            for event in events:
                event()

    partials(
        0,
        v_mate,
        (v_events[10:12], dv_events[:2], dv_events[2:4] + v_events[12:13], v_events[13:14], ()),
    )
    v_events[14]()
    v_end()

    def spread(s, wide, thin):
        values = vall[tiles[s]]
        wide[...] = nt(gs[s], values)
        thin[...] = nn(probs[s], values).astype(BF16)

    def backward(s, wide, thin, mid):
        attn_f = thin[...].astype(F32)
        delta = jnp.sum(gs[s].astype(F32) * attn_f, axis=1, keepdims=True)
        mid[...] = (probs[s].astype(F32) * (wide[...] - delta) * scale).astype(BF16)
        product = cs[s].astype(F32) * attn_f
        cs[s] = thin[...]
        gacc[...] += sum(product[8 * i : 8 * i + 8] for i in range(heads * span_len // 8))

    def key_alone(s, mid):
        dscore = mid[...]
        alone[s] = tn(qs[s], dscore).astype(BF16)
        qs[s] = nn(dscore, kall[tiles[jnp.minimum(s, cap)]]).astype(BF16)

    def backward_two(i, carry):
        spread(2 * i + 1, wide_b, thin_b)
        key_alone(before(i), mid_b)
        backward(2 * i, wide_a, thin_a, mid_a)
        spread(jnp.minimum(2 * i + 2, cap), wide_a, thin_a)
        key_alone(2 * i, mid_a)
        backward(2 * i + 1, wide_b, thin_b, mid_b)
        return carry

    spread(0, wide_a, thin_a)
    run(
        backward_two,
        spans // 2,
        (
            (2, dv_events[4:6]),
            (4, dv_events[6:8]),
            (7, dv_events[8:9]),
            (11, dv_events[9:11]),
            (14, dv_events[11:12]),
            (16, ()),
        ),
    )
    pl.semaphore_signal(free, inc=1, device_id=(mate, my), device_id_type=MESH)
    gate_begin(0, gacc[...])
    key_alone(cap, mid_b)
    rows_out = by_head(att_hbm, cs, 4, True) + by_head(dq_hbm, qs, 4 + heads, True)
    for copy in rows_out:
        copy.start()

    pl.semaphore_wait(free, 1)
    dv_out = []

    def dv_done():
        dv_last()
        dv_out.append(finish(0, dv_hbm, 2))

    partials(
        1,
        k_mate,
        (
            [dv_done],
            [lambda: gate_begin(1, gate_end(0))] + dk_events[:2],
            dk_events[2:4],
            [lambda: gate_begin(2, gate_end(1))],
            [],
        ),
    )
    flush()
    for event in dk_events[4:6]:
        event()
    gate_begin(3, gate_end(2))
    for event in dk_events[6:8]:
        event()
    dk_events[8]()
    dk_events[9]()
    grand = jnp.sum(gate_end(3))
    slope = (1.0 - gate_tanh * gate_tanh) * grand / math.sqrt(total_elems)
    gate_out[0] = slope[0, 0]
    for event in dk_events[10:]:
        event()
    flush()

    def drain(p, carry):
        v_mate(p).wait_send()
        k_mate(p).wait_send()
        return carry

    lax.fori_loop(0, spans // 2, drain, 0)
    dk_last()
    dk_out = finish(1, dk_hbm, 3)
    flush()
    for copy in rows_out + [dk_out] + dv_out:
        copy.wait()


def body(queries, image_keys, image_values, span_tiles, gate_logit, cotangent):
    tok_count, columns = queries.shape
    spans = span_tiles.shape[0]
    span_len = tok_count // spans
    heads = columns // HEAD
    image_len = image_keys.shape[1]
    tile_count = lax.axis_size("seq")
    total_elems = tok_count * tile_count * columns * lax.axis_size("mp")
    smem = pl.BlockSpec(memory_space=pltpu.SMEM)
    hbm = pl.BlockSpec(memory_space=pl.ANY)
    sizes = (spans, span_len, heads, image_len, total_elems)
    rows = heads * span_len
    kv = (tile_count, image_len, HEAD)
    by_span = (spans, span_len, columns)
    att, dq, dk, dv, gate = pl.pallas_call(
        functools.partial(kernel, sizes),
        out_shape=(
            jax.ShapeDtypeStruct(by_span, BF16),
            jax.ShapeDtypeStruct(by_span, BF16),
            jax.ShapeDtypeStruct(image_keys.shape, BF16),
            jax.ShapeDtypeStruct(image_values.shape, BF16),
            jax.ShapeDtypeStruct((1,), F32),
        ),
        in_specs=[smem, smem, hbm, hbm, hbm, hbm],
        out_specs=(hbm, hbm, hbm, hbm, smem),
        scratch_shapes=[
            pltpu.VMEM(kv, BF16),
            pltpu.VMEM(kv, BF16),
            pltpu.VMEM((spans, rows, image_len), BF16),
            pltpu.VMEM((spans, rows, HEAD), BF16),
            pltpu.VMEM((spans + 1, rows, HEAD), BF16),
            pltpu.VMEM((spans, rows, HEAD), BF16),
            pltpu.VMEM((spans + 1, HEAD, image_len), BF16),
            pltpu.VMEM((2, tile_count, HEAD, image_len), BF16),
            pltpu.VMEM((2, HEAD), jnp.int32),
            pltpu.SMEM((2, HEAD), jnp.int32),
            pltpu.VMEM((tile_count // 2, 2, HEAD // 2, image_len), BF16),
            pltpu.VMEM((2, RING, 2, 2, HEAD // 4, image_len), BF16),
            pltpu.VMEM((2, RING, 2, 2, HEAD // 2, image_len), BF16),
            pltpu.VMEM((2, 2, 2, HEAD // 4, image_len), BF16),
            pltpu.VMEM((2, 2, 2, HEAD // 2, image_len), BF16),
            pltpu.VMEM((2, HEAD // 2, image_len), BF16),
            pltpu.VMEM((2, image_len, HEAD), BF16),
            pltpu.VMEM((rows, image_len), F32),
            pltpu.VMEM((rows, image_len), F32),
            pltpu.VMEM((rows, HEAD), BF16),
            pltpu.VMEM((rows, HEAD), BF16),
            pltpu.VMEM((rows, image_len), BF16),
            pltpu.VMEM((rows, image_len), BF16),
            pltpu.VMEM((8, HEAD), F32),
            pltpu.VMEM((4, RING, 8, HEAD), F32),
            pltpu.SemaphoreType.DMA((180,)),
            pltpu.SemaphoreType.DMA((180,)),
            pltpu.SemaphoreType.DMA((4 + 2 * heads,)),
            pltpu.SemaphoreType.REGULAR,
        ],
        compiler_params=pltpu.CompilerParams(
            collective_id=0, has_side_effects=True, vmem_limit_bytes=67043328
        ),
        name="cross_attention",
    )(
        span_tiles.reshape(spans),
        gate_logit,
        queries.reshape(by_span),
        image_keys,
        image_values,
        cotangent.reshape(by_span),
    )
    gate_tanh = jnp.tanh(gate_logit[0])
    attended = (gate_tanh * att.reshape(queries.shape).astype(F32)).astype(BF16)
    return (attended, dq.reshape(queries.shape), dk, dv, gate)


def solution(mesh):
    placed = (
        P("seq", "mp"),
        P("seq", None, "mp"),
        P("seq", None, "mp"),
        P("seq", None),
        P(),
        P("seq", "mp"),
    )
    return jax.shard_map(
        body,
        mesh=mesh,
        in_specs=placed,
        out_specs=(P("seq", "mp"), P("seq", "mp"), P("seq", None, "mp"), P("seq", None, "mp"), P()),
        check_vma=False,
    )
```

time: 134 us -> 111 us (0.83)
  Pallas kernels: 122 us -> 101 us
  local copies, waits for them, and re-layouts: 9.22 us -> 2.68 us
  other arithmetic: 1.32 us -> 3.65 us
  between operations: 1.29 us -> 3.1 us
    pallas_call x1, Pallas kernels: 122 us -> 101 us  [body(): pl.pallas_call(functools.partial(kernel, sizes), out_shape=(jax.ShapeDtyp...]
    unnamed x6 -> x9, local copies, waits for them, and re-layouts: 8.03 us -> 2.68 us
    convert_element_type x0 -> x1, other arithmetic: none -> 3.65 us  [body(): attended = (gate_tanh * att.reshape(queries.shape).astype(F32)).astype(BF16)]
where the time goes in v2:
time: 111 us
  Pallas kernels  101 us (91%)
  other arithmetic  3.65 us (3%)
  between operations  3.1 us (3%)
  local copies, waits for them, and re-layouts  2.68 us (2%)
    pallas_call x1, Pallas kernels, body(): pl.pallas_call(functools.partial(kernel, sizes), out_shape=(jax.ShapeDtyp...  101 us
    convert_element_type x1, other arithmetic, body(): attended = (gate_tanh * att.reshape(queries.shape).astype(F32)).astype(BF16)  3.65 us
    unnamed x9, local copies, waits for them, and re-layouts  2.68 us

profile of v2, /device:TPU:1, one launch (start us, length us, event | category | flops | bytes accessed | tf_op | source)
XLA Modules:
  0.0 110.6 jit_solution(8569610769565325661)
XLA Ops:
  1.3 101.2 %cross_attention.1 = (bf16[32,32,1024]{2,1,0:T(8,128)(2,1)}, bf16[32,32,1024]{2,1,0:T(8,128)(2,1)}, bf16[1,768,128]{2,1,0:T(8,128)(2,1)}, bf16[1,768,128]{2,1,0:T(8,128)(2,1)}, f32[1]{0:T(128)}) custom-call(s32[32]{0:T(128)} %bitcast.10, f32[1]{0:T(128)S(6)} %copy.15.gate, bf16[32,32,1024]{2,1,0:T(8,128)(2,1)} %bitcast.6, bf16[1,768,128]{2,1,0:T(8,128)(2,1)} %k_hbm.1, ...), custom_call_target="tpu_custom_call" | custom-call | tf_op jit(solution)/shard_map/cross_attention/pallas_call | solution.py:638
  102.5 0.0 copy-start
  102.5 3.6 %multiply_convert_fusion = bf16[32,32,1024]{2,1,0:T(8,128)(2,1)} fusion(bf16[32,32,1024]{2,1,0:T(8,128)(2,1)} %get-tuple-element.10, f32[]{:T(128)} %bitcast), kind=kLoop, calls=%fused_computation | loop fusion | flops 3145728 | bytes 4194308 | tf_op jit(solution)/shard_map/convert_element_type | solution.py:693
  106.2 0.0 copy-done
  106.2 0.0 copy-start.2
  106.2 0.0 copy-start.1
  106.2 1.3 %copy.16 = bf16[1024,1024]{1,0:T(8,128)(2,1)} copy(bf16[1024,1024]{1,0:T(8,128)(2,1)S(1)} %bitcast.9) | data formatting | bytes 4194304
  107.5 0.0 copy-done.2
  107.5 0.7 copy.17
  108.2 0.0 copy-done.1
  108.2 0.7 copy.18
Async XLA Ops:
  102.5 3.7 %copy-start = (bf16[32,32,1024]{2,1,0:T(8,128)(2,1)S(1)}, bf16[32,32,1024]{2,1,0:T(8,128)(2,1)}, u32[]{:S(2)}) copy-start(bf16[32,32,1024]{2,1,0:T(8,128)(2,1)} %get-tuple-element.11) | copy-start | bytes 6291460
  106.2 1.3 %copy-start.2 = (bf16[1,768,128]{2,1,0:T(8,128)(2,1)S(1)}, bf16[1,768,128]{2,1,0:T(8,128)(2,1)}, u32[]{:S(2)}) copy-start(bf16[1,768,128]{2,1,0:T(8,128)(2,1)} %get-tuple-element.22) | copy-start | bytes 589828
  106.2 2.0 %copy-start.1 = (bf16[1,768,128]{2,1,0:T(8,128)(2,1)S(1)}, bf16[1,768,128]{2,1,0:T(8,128)(2,1)}, u32[]{:S(2)}) copy-start(bf16[1,768,128]{2,1,0:T(8,128)(2,1)} %get-tuple-element.23) | copy-start | bytes 589828

commit v3 on v2

--- a/solution.py
+++ b/solution.py
@@ -576,6 +576,8 @@
         copy.start()
 
     pl.semaphore_wait(free, 1)
+    settled = list(started)
+    started.clear()
     dv_out = []
 
     def dv_done():
@@ -593,7 +595,8 @@
             [],
         ),
     )
-    flush()
+    for make in settled:
+        make().wait_send()
     for event in dk_events[4:6]:
         event()
     gate_begin(3, gate_end(2))
@@ -606,7 +609,6 @@
     gate_out[0] = slope[0, 0]
     for event in dk_events[10:]:
         event()
-    flush()
 
     def drain(p, carry):
         v_mate(p).wait_send()

time: 111 us -> 110 us (level)
  no operation moved by 1% of the time
where the time goes in v3:
time: 110 us
  Pallas kernels  100 us (91%)
  other arithmetic  3.65 us (3%)
  between operations  3.1 us (3%)
  local copies, waits for them, and re-layouts  2.68 us (2%)
    pallas_call x1, Pallas kernels, body(): pl.pallas_call(functools.partial(kernel, sizes), out_shape=(jax.ShapeDtyp...  100 us
    convert_element_type x1, other arithmetic, body(): attended = (gate_tanh * att.reshape(queries.shape).astype(F32)).astype(BF16)  3.65 us
    unnamed x9, local copies, waits for them, and re-layouts  2.68 us

profile of v3, /device:TPU:1, one launch (start us, length us, event | category | flops | bytes accessed | tf_op | source)
XLA Modules:
  0.0 109.5 jit_solution(14797939950277050641)
XLA Ops:
  1.3 100.1 %cross_attention.1 = (bf16[32,32,1024]{2,1,0:T(8,128)(2,1)}, bf16[32,32,1024]{2,1,0:T(8,128)(2,1)}, bf16[1,768,128]{2,1,0:T(8,128)(2,1)}, bf16[1,768,128]{2,1,0:T(8,128)(2,1)}, f32[1]{0:T(128)}) custom-call(s32[32]{0:T(128)} %bitcast.10, f32[1]{0:T(128)S(6)} %copy.15.gate, bf16[32,32,1024]{2,1,0:T(8,128)(2,1)} %bitcast.6, bf16[1,768,128]{2,1,0:T(8,128)(2,1)} %k_hbm.1, ...), custom_call_target="tpu_custom_call" | custom-call | tf_op jit(solution)/shard_map/cross_attention/pallas_call | solution.py:640
  101.4 0.0 copy-start
  101.4 3.6 %multiply_convert_fusion = bf16[32,32,1024]{2,1,0:T(8,128)(2,1)} fusion(bf16[32,32,1024]{2,1,0:T(8,128)(2,1)} %get-tuple-element.10, f32[]{:T(128)} %bitcast), kind=kLoop, calls=%fused_computation | loop fusion | flops 3145728 | bytes 4194308 | tf_op jit(solution)/shard_map/convert_element_type | solution.py:695
  105.1 0.0 copy-done
  105.1 0.0 copy-start.2
  105.1 0.0 copy-start.1
  105.1 1.3 %copy.16 = bf16[1024,1024]{1,0:T(8,128)(2,1)} copy(bf16[1024,1024]{1,0:T(8,128)(2,1)S(1)} %bitcast.9) | data formatting | bytes 4194304
  106.4 0.0 copy-done.2
  106.4 0.7 copy.17
  107.1 0.0 copy-done.1
  107.1 0.7 copy.18
Async XLA Ops:
  101.4 3.7 %copy-start = (bf16[32,32,1024]{2,1,0:T(8,128)(2,1)S(1)}, bf16[32,32,1024]{2,1,0:T(8,128)(2,1)}, u32[]{:S(2)}) copy-start(bf16[32,32,1024]{2,1,0:T(8,128)(2,1)} %get-tuple-element.11) | copy-start | bytes 6291460
  105.1 1.3 %copy-start.2 = (bf16[1,768,128]{2,1,0:T(8,128)(2,1)S(1)}, bf16[1,768,128]{2,1,0:T(8,128)(2,1)}, u32[]{:S(2)}) copy-start(bf16[1,768,128]{2,1,0:T(8,128)(2,1)} %get-tuple-element.22) | copy-start | bytes 589828
  105.1 2.0 %copy-start.1 = (bf16[1,768,128]{2,1,0:T(8,128)(2,1)S(1)}, bf16[1,768,128]{2,1,0:T(8,128)(2,1)}, u32[]{:S(2)}) copy-start(bf16[1,768,128]{2,1,0:T(8,128)(2,1)} %get-tuple-element.23) | copy-start | bytes 589828

commit v4 on v3

--- a/solution.py
+++ b/solution.py
@@ -538,7 +538,7 @@
         delta = jnp.sum(gs[s].astype(F32) * attn_f, axis=1, keepdims=True)
         mid[...] = (probs[s].astype(F32) * (wide[...] - delta) * scale).astype(BF16)
         product = cs[s].astype(F32) * attn_f
-        cs[s] = thin[...]
+        cs[s] = (tanh_row * attn_f).astype(BF16)
         gacc[...] += sum(product[8 * i : 8 * i + 8] for i in range(heads * span_len // 8))
 
     def key_alone(s, mid):
@@ -691,9 +691,7 @@
         image_values,
         cotangent.reshape(by_span),
     )
-    gate_tanh = jnp.tanh(gate_logit[0])
-    attended = (gate_tanh * att.reshape(queries.shape).astype(F32)).astype(BF16)
-    return (attended, dq.reshape(queries.shape), dk, dv, gate)
+    return (att.reshape(queries.shape), dq.reshape(queries.shape), dk, dv, gate)
 
 
 def solution(mesh):

time: 110 us -> 109 us (level)
  other arithmetic: 3.65 us -> 0 us
  local copies, waits for them, and re-layouts: 2.68 us -> 5.91 us
    convert_element_type x1 -> x0, other arithmetic: 3.65 us -> none  [body(): attended = (gate_tanh * att.reshape(queries.shape).astype(F32)).astype(BF16)]
    unnamed x9 -> x10, local copies, waits for them, and re-layouts: 2.68 us -> 5.91 us
where the time goes in v4:
time: 109 us
  Pallas kernels  100 us (92%)
  local copies, waits for them, and re-layouts  5.91 us (5%)
  between operations  3.06 us (3%)
    pallas_call x1, Pallas kernels, body(): pl.pallas_call(functools.partial(kernel, sizes), out_shape=(jax.ShapeDtyp...  100 us
    unnamed x10, local copies, waits for them, and re-layouts  5.91 us

profile of v4, /device:TPU:1, one launch (start us, length us, event | category | flops | bytes accessed | tf_op | source)
XLA Modules:
  0.0 109.0 jit_solution(6780914841184326692)
XLA Ops:
  1.3 100.0 %cross_attention.1 = (bf16[32,32,1024]{2,1,0:T(8,128)(2,1)}, bf16[32,32,1024]{2,1,0:T(8,128)(2,1)}, bf16[1,768,128]{2,1,0:T(8,128)(2,1)}, bf16[1,768,128]{2,1,0:T(8,128)(2,1)}, f32[1]{0:T(128)}) custom-call(s32[32]{0:T(128)} %bitcast.9, f32[1]{0:T(128)S(6)} %copy.16.gate, bf16[32,32,1024]{2,1,0:T(8,128)(2,1)} %bitcast.5, bf16[1,768,128]{2,1,0:T(8,128)(2,1)} %k_hbm.1, ...), custom_call_target="tpu_custom_call" | custom-call | tf_op jit(solution)/shard_map/cross_attention/pallas_call | solution.py:640
  101.3 0.0 copy-start
  101.3 3.2 %copy.17 = bf16[1024,1024]{1,0:T(8,128)(2,1)} copy(bf16[1024,1024]{1,0:T(8,128)(2,1)} %bitcast.8) | data formatting | bytes 4194304
  104.6 0.0 copy-done
  104.6 0.0 copy-start.2
  104.6 0.0 copy-start.1
  104.6 1.3 %copy.18 = bf16[1024,1024]{1,0:T(8,128)(2,1)} copy(bf16[1024,1024]{1,0:T(8,128)(2,1)S(1)} %bitcast.7) | data formatting | bytes 4194304
  105.9 0.0 copy-done.2
  105.9 0.7 copy.19
  106.6 0.0 copy-done.1
  106.6 0.7 copy.20
Async XLA Ops:
  101.3 3.2 %copy-start = (bf16[32,32,1024]{2,1,0:T(8,128)(2,1)S(1)}, bf16[32,32,1024]{2,1,0:T(8,128)(2,1)}, u32[]{:S(2)}) copy-start(bf16[32,32,1024]{2,1,0:T(8,128)(2,1)} %get-tuple-element.11) | copy-start | bytes 6291460
  104.6 1.3 %copy-start.2 = (bf16[1,768,128]{2,1,0:T(8,128)(2,1)S(1)}, bf16[1,768,128]{2,1,0:T(8,128)(2,1)}, u32[]{:S(2)}) copy-start(bf16[1,768,128]{2,1,0:T(8,128)(2,1)} %get-tuple-element.22) | copy-start | bytes 589828
  104.6 2.0 %copy-start.1 = (bf16[1,768,128]{2,1,0:T(8,128)(2,1)S(1)}, bf16[1,768,128]{2,1,0:T(8,128)(2,1)}, u32[]{:S(2)}) copy-start(bf16[1,768,128]{2,1,0:T(8,128)(2,1)} %get-tuple-element.23) | copy-start | bytes 589828

commit v5 on v4

--- a/solution.py
+++ b/solution.py
@@ -604,11 +604,11 @@
         event()
     dk_events[8]()
     dk_events[9]()
+    for event in dk_events[10:]:
+        event()
     grand = jnp.sum(gate_end(3))
     slope = (1.0 - gate_tanh * gate_tanh) * grand / math.sqrt(total_elems)
     gate_out[0] = slope[0, 0]
-    for event in dk_events[10:]:
-        event()
 
     def drain(p, carry):
         v_mate(p).wait_send()

time: 109 us -> 109 us (level)
  no operation moved by 1% of the time
where the time goes in v5:
time: 109 us
  Pallas kernels  99.9 us (92%)
  local copies, waits for them, and re-layouts  5.91 us (5%)
  between operations  3.06 us (3%)
    pallas_call x1, Pallas kernels, body(): pl.pallas_call(functools.partial(kernel, sizes), out_shape=(jax.ShapeDtyp...  99.9 us
    unnamed x10, local copies, waits for them, and re-layouts  5.91 us

profile of v5, /device:TPU:1, one launch (start us, length us, event | category | flops | bytes accessed | tf_op | source)
XLA Modules:
  0.0 108.9 jit_solution(12839286770978641667)
XLA Ops:
  1.3 99.9 %cross_attention.1 = (bf16[32,32,1024]{2,1,0:T(8,128)(2,1)}, bf16[32,32,1024]{2,1,0:T(8,128)(2,1)}, bf16[1,768,128]{2,1,0:T(8,128)(2,1)}, bf16[1,768,128]{2,1,0:T(8,128)(2,1)}, f32[1]{0:T(128)}) custom-call(s32[32]{0:T(128)} %bitcast.9, f32[1]{0:T(128)S(6)} %copy.16.gate, bf16[32,32,1024]{2,1,0:T(8,128)(2,1)} %bitcast.5, bf16[1,768,128]{2,1,0:T(8,128)(2,1)} %k_hbm.1, ...), custom_call_target="tpu_custom_call" | custom-call | tf_op jit(solution)/shard_map/cross_attention/pallas_call | solution.py:640
  101.2 0.0 copy-start
  101.2 3.2 %copy.17 = bf16[1024,1024]{1,0:T(8,128)(2,1)} copy(bf16[1024,1024]{1,0:T(8,128)(2,1)} %bitcast.8) | data formatting | bytes 4194304
  104.4 0.0 copy-done
  104.4 0.0 copy-start.2
  104.4 0.0 copy-start.1
  104.4 1.3 %copy.18 = bf16[1024,1024]{1,0:T(8,128)(2,1)} copy(bf16[1024,1024]{1,0:T(8,128)(2,1)S(1)} %bitcast.7) | data formatting | bytes 4194304
  105.7 0.0 copy-done.2
  105.7 0.7 copy.19
  106.4 0.0 copy-done.1
  106.4 0.7 copy.20
Async XLA Ops:
  101.2 3.2 %copy-start = (bf16[32,32,1024]{2,1,0:T(8,128)(2,1)S(1)}, bf16[32,32,1024]{2,1,0:T(8,128)(2,1)}, u32[]{:S(2)}) copy-start(bf16[32,32,1024]{2,1,0:T(8,128)(2,1)} %get-tuple-element.11) | copy-start | bytes 6291460
  104.4 1.3 %copy-start.2 = (bf16[1,768,128]{2,1,0:T(8,128)(2,1)S(1)}, bf16[1,768,128]{2,1,0:T(8,128)(2,1)}, u32[]{:S(2)}) copy-start(bf16[1,768,128]{2,1,0:T(8,128)(2,1)} %get-tuple-element.22) | copy-start | bytes 589828
  104.4 2.0 %copy-start.1 = (bf16[1,768,128]{2,1,0:T(8,128)(2,1)S(1)}, bf16[1,768,128]{2,1,0:T(8,128)(2,1)}, u32[]{:S(2)}) copy-start(bf16[1,768,128]{2,1,0:T(8,128)(2,1)} %get-tuple-element.23) | copy-start | bytes 589828
